TPU v7x, 256 devices: a whole 4x4x8 slice. The times are simulated.
256 devices in a mesh: section: 16 (over x, y), seq: 16 (over z, core).
Axes of the slice: x: 4, y: 4, z: 8, core: 2. Of those that a mesh axis runs over, the one named last changes fastest.
Arguments:
- inputs: bfloat16 [4, 8192, 1536], P(None, 'seq'), may hold values from -40 to 40
- weights: bfloat16 [2, 5, 1536, 1536], P(None, None, None, 'section'), may hold values from -0.0625 to 0.0625
- gains: float32 [2, 1536], replicated, may hold values from 0.1 to 1.9
Outputs:
- activations: bfloat16 [2, 4, 8192, 1536], P(None, None, 'seq', 'section')
All inputs are finite; a program needn't handle non-finite values.
Results may differ from a plain program's by a relative error of at most 0.0044.
Values may be sent and summed in bfloat16 or wider, within the bound.
No kernel may reach another device: no remote copies, remote signals or barrier semaphores. Data moves between devices by JAX's collectives and lax.ppermute only.
A program may use at most 128 MiB of HBM per device.

v0:
```python
import jax
import jax.numpy as jnp
from jax import lax
from jax.sharding import PartitionSpec as P


def with_halo(value, sides, width):
    for axis, dim in sides:
        count, length = (lax.axis_size(axis), value.shape[dim])
        up = [(i, (i + 1) % count) for i in range(count - 1)]
        down = [(j, i) for i, j in up]
        last = lax.slice_in_dim(value, length - width, length, axis=dim)
        initial = lax.slice_in_dim(value, 0, width, axis=dim)
        before = lax.ppermute(last, axis, up)
        after = lax.ppermute(initial, axis, down)
        value = jnp.concatenate([before, value, after], axis=dim)
    return value


def convolve(padded, kernel):
    count = padded.shape[1] - 4
    total = jnp.zeros((padded.shape[0], count, kernel.shape[2]), jnp.float32)
    for k in range(5):
        total = total + jnp.einsum(
            "brc,co->bro", padded[:, k : k + count], kernel[k], preferred_element_type=jnp.float32
        )
    return total


def normed(current, gain):
    values = current.astype(jnp.float32)
    scale = lax.rsqrt(jnp.mean(values * values, axis=-1, keepdims=True) + 1e-06)
    return jax.nn.gelu(values * scale * gain).astype(jnp.bfloat16)


def neighbours(hidden):
    return with_halo(hidden, (("seq", 1),), 2)


def local(inputs, weights, gains):
    share = weights.shape[3]
    begin = lax.axis_index("section") * share
    hidden = normed(inputs, gains[0])
    conv = convolve(neighbours(hidden), weights[0])
    own = lax.dynamic_slice_in_dim(inputs, begin, share, 2)
    current = (own.astype(jnp.float32) + conv).astype(jnp.bfloat16)
    results = [current]
    kernel = weights[1]
    whole = lax.all_gather(current, "section", axis=2, tiled=True)
    conv = convolve(neighbours(normed(whole, gains[1])), kernel)
    current = (current.astype(jnp.float32) + conv).astype(jnp.bfloat16)
    results.append(current)
    return jnp.stack(results, axis=0)


def solution(mesh):
    in_specs = (P(None, "seq", None), P(None, None, None, "section"), P())
    out_specs = P(None, None, "seq", "section")
    return jax.shard_map(local, mesh=mesh, in_specs=in_specs, out_specs=out_specs, check_vma=False)
```

profile of v0, /device:TPU:1, one launch (start us, length us, event | category | flops | bytes accessed | tf_op | source)
XLA Modules:
  0.0 165.4 jit_solution(3972784400976625223)
XLA Ops:
  6.5 4.2 %fusion = f32[4,512]{1,0:T(4,128)S(1)} fusion(bf16[4,512,1536]{2,1,0:T(8,128)(2,1)} %param.3), kind=kLoop, calls=%fused_computation.6 | loop fusion | flops 9435136 | bytes 6299648 | tf_op jit(solution)/shard_map/reduce_sum | solution.py:32
  11.2 5.8 %fusion.4 = bf16[4,512,1536]{2,1,0:T(8,128)(2,1)S(1)} fusion(bf16[4,512,1536]{2,1,0:T(8,128)(2,1)S(1)} %copy-done.1, f32[1536]{0:T(1024)S(1)} %get-tuple-element.6, f32[4,512]{1,0:T(4,128)S(1)} %add_rsqrt_fusion.1), kind=kLoop, calls=%fused_computation.10 | loop fusion | flops 37748736 | bytes 12597248 | tf_op jit(solution)/shard_map/convert_element_type | solution.py:33
  16.9 2.7 %copy-done.2 = bf16[4,512,1536]{2,1,0:T(8,128)(2,1)} copy-done((bf16[4,512,1536]{2,1,0:T(8,128)(2,1)}, bf16[4,512,1536]{2,1,0:T(8,128)(2,1)S(1)}, u32[]{:S(2)}) %copy-start.2) | copy-done | bytes 6291480
  19.6 4.9 %collective-permute-start = (bf16[4,2,1536]{2,1,0:T(2,128)(2,1)S(1)}, bf16[4,2,1536]{2,1,0:T(2,128)(2,1)S(1)}, u32[]{:S(2)}, u32[]{:S(2)}) collective-permute-start(bf16[4,2,1536]{2,1,0:T(2,128)(2,1)S(1)} %get-tuple-element.9), channel_id=1, source_target_pairs={{0,1},{1,2},{2,3},{3,4},{4,5},{5,6},{6,7},{7,8},{8,9},{9,10},{10,1... | collective-permute-start | bytes 73736 | tf_op jit(solution)/shard_map/ppermute | solution.py:14
  24.6 2.1 %collective-permute-start.1 = (bf16[4,2,1536]{2,1,0:T(2,128)(2,1)S(1)}, bf16[4,2,1536]{2,1,0:T(2,128)(2,1)S(1)}, u32[]{:S(2)}, u32[]{:S(2)}) collective-permute-start(bf16[4,2,1536]{2,1,0:T(2,128)(2,1)S(1)} %get-tuple-element.10), channel_id=1, source_target_pairs={{1,0},{2,1},{3,2},{4,3},{5,4},{6,5},{7,6},{8,7},{9,8},{10,9},{11,1... | collective-permute-start | bytes 73736 | tf_op jit(solution)/shard_map/ppermute | solution.py:15
  26.7 4.8 %fusion.83 = f32[4,512,96]{1,2,0:T(8,128)S(1)} fusion(bf16[4,512,1536]{2,1,0:T(8,128)(2,1)} %copy-done.2, bf16[2,5,1536,96]{2,3,1,0:T(8,128)(2,1)} %param.4), kind=kOutput, calls=%fused_computation.75 | convolution fusion | flops 603979776 | bytes 7372800 | tf_op jit(solution)/shard_map/brc,co->bro/dot_general | solution.py:24
  31.5 1.5 constant_dynamic-slice_fusion
  33.0 1.0 copy.18
  33.9 4.8 %fusion.28 = f32[4,512,96]{1,2,0:T(8,128)S(1)} fusion(bf16[4,2,1536]{2,1,0:T(2,128)(2,1)S(1)} %collective-permute-done.1, bf16[4,512,1536]{2,1,0:T(8,128)(2,1)} %copy-done.2, bf16[2,5,1536,96]{2,3,1,0:T(8,128)(2,1)} %param.4), kind=kOutput, calls=%fused_computation.45 | convolution fusion | flops 616562688 | bytes 7397376 | tf_op jit(solution)/shard_map/brc,co->bro/dot_general | solution.py:24
  38.8 3.0 %fusion.30 = f32[4,512,96]{1,2,0:T(8,128)S(1)} fusion(bf16[4,512,1536]{2,1,0:T(8,128)(2,1)S(1)} %bitcast.58, bf16[4,2,1536]{2,1,0:T(2,128)(2,1)S(1)} %collective-permute-done, bf16[2,5,1536,96]{2,3,1,0:T(8,128)(2,1)} %param.4), kind=kOutput, calls=%fused_computation.48 | convolution fusion | flops 616562688 | bytes 7397376 | tf_op jit(solution)/shard_map/brc,co->bro/dot_general | solution.py:24
  41.8 3.1 %fusion.64 = f32[4,512,96]{1,2,0:T(8,128)S(1)} fusion(f32[4,512,96]{1,2,0:T(8,128)S(1)} %fusion.83, f32[4,512,96]{1,2,0:T(8,128)S(1)} %fusion.30, bf16[4,2,1536]{2,1,0:T(2,128)(2,1)S(1)} %collective-permute-done, bf16[4,512,1536]{2,1,0:T(8,128)(2,1)S(1)} %bitcast.58, bf16[2,5,1536,96]{2,3,1,0:T(8,128)(2,1)} %param.4), kind=kOutput, calls=%fused_computation.62 | convolution fusion | flops 616955904 | bytes 8970240 | tf_op jit(solution)/shard_map/brc,co->bro/dot_general | solution.py:24
  44.9 3.5 %fusion.67 = bf16[4,512,96]{1,2,0:T(8,128)(2,1)S(1)} fusion(f32[4,512,96]{1,2,0:T(8,128)S(1)} %fusion.28, f32[4,512,96]{1,2,0:T(8,128)S(1)} %fusion.64, bf16[4,512,1536]{2,1,0:T(8,128)(2,1)S(1)} %bitcast.58, bf16[4,2,1536]{2,1,0:T(2,128)(2,1)S(1)} %collective-permute-done.1, bf16[4,512,96]{1,2,0:T(8,128)(2,1)S(1)} %copy-done.3, ...), kind=kOutput, calls=%fused_computation.63 | convolution fusion | flops 617545728 | bytes 8970240 | tf_op jit(solution)/shard_map/brc,co->bro/dot_general | solution.py:24
  48.4 1.1 copy.16
  49.5 70.2 %all-gather.2.cloned.1.call-done = bf16[4,512,1536]{1,0,2:T(4,128)(2,1)} async-done(((bf16[4,512,96]{1,0,2:T(4,128)(2,1)}), bf16[4,512,1536]{1,0,2:T(4,128)(2,1)}) %all-gather.2.cloned.1.call-update) | async-done | bytes 6291472 | tf_op jit(solution)/shard_map/all_gather | solution.py:49
  119.7 10.6 %copy.17 = bf16[4,512,1536]{2,1,0:T(8,128)(2,1)} copy(bf16[4,512,1536]{1,0,2:T(4,128)(2,1)} %all-gather.2.cloned.1.call-done) | data formatting | bytes 12582912 | tf_op jit(solution)/shard_map/all_gather | solution.py:49
  130.3 4.2 %fusion.9 = f32[4,512]{1,0:T(4,128)S(1)} fusion(bf16[4,512,1536]{2,1,0:T(8,128)(2,1)} %copy.17), kind=kLoop, calls=%fused_computation.15 | loop fusion | flops 9435136 | bytes 6299648 | tf_op jit(solution)/shard_map/reduce_sum | solution.py:32
  134.9 5.8 %fusion.13 = bf16[4,512,1536]{2,1,0:T(8,128)(2,1)S(1)} fusion(bf16[4,512,1536]{2,1,0:T(8,128)(2,1)S(1)} %copy-done, f32[1536]{0:T(1024)S(1)} %get-tuple-element.5, f32[4,512]{1,0:T(4,128)S(1)} %add_rsqrt_fusion), kind=kLoop, calls=%fused_computation.19 | loop fusion | flops 37748736 | bytes 12597248 | tf_op jit(solution)/shard_map/convert_element_type | solution.py:33
  140.8 2.6 %collective-permute-start.3 = (bf16[4,2,1536]{2,1,0:T(2,128)(2,1)S(1)}, bf16[4,2,1536]{2,1,0:T(2,128)(2,1)S(1)}, u32[]{:S(2)}, u32[]{:S(2)}) collective-permute-start(bf16[4,2,1536]{2,1,0:T(2,128)(2,1)S(1)} %get-tuple-element.8), channel_id=1, source_target_pairs={{1,0},{2,1},{3,2},{4,3},{5,4},{6,5},{7,6},{8,7},{9,8},{10,9},{11,1... | collective-permute-start | bytes 73736 | tf_op jit(solution)/shard_map/ppermute | solution.py:15
  143.4 2.0 %fusion.77 = f32[4,512,96]{1,2,0:T(8,128)S(1)} fusion(bf16[4,512,1536]{2,1,0:T(8,128)(2,1)S(1)} %fusion.13, bf16[2,5,1536,96]{2,3,1,0:T(8,128)(2,1)S(1)} %copy-done.4), kind=kOutput, calls=%fused_computation.69 | convolution fusion | flops 603979776 | bytes 7372800 | tf_op jit(solution)/shard_map/brc,co->bro/dot_general | solution.py:24
  145.4 3.3 %collective-permute-start.2 = (bf16[4,2,1536]{2,1,0:T(2,128)(2,1)S(1)}, bf16[4,2,1536]{2,1,0:T(2,128)(2,1)S(1)}, u32[]{:S(2)}, u32[]{:S(2)}) collective-permute-start(bf16[4,2,1536]{2,1,0:T(2,128)(2,1)S(1)} %get-tuple-element.7), channel_id=1, source_target_pairs={{0,1},{1,2},{2,3},{3,4},{4,5},{5,6},{6,7},{7,8},{8,9},{9,10},{10,1... | collective-permute-start | bytes 73736 | tf_op jit(solution)/shard_map/ppermute | solution.py:14
  148.7 2.1 %fusion.24 = f32[4,512,96]{1,2,0:T(8,128)S(1)} fusion(bf16[4,2,1536]{2,1,0:T(2,128)(2,1)S(1)} %collective-permute-done.3, bf16[4,512,1536]{2,1,0:T(8,128)(2,1)S(1)} %fusion.13, bf16[2,5,1536,96]{2,3,1,0:T(8,128)(2,1)S(1)} %copy-done.4), kind=kOutput, calls=%fused_computation.39 | convolution fusion | flops 616562688 | bytes 7397376 | tf_op jit(solution)/shard_map/brc,co->bro/dot_general | solution.py:24
  150.8 2.1 %fusion.26 = f32[4,512,96]{1,2,0:T(8,128)S(1)} fusion(bf16[4,512,1536]{2,1,0:T(8,128)(2,1)S(1)} %fusion.13, bf16[4,2,1536]{2,1,0:T(2,128)(2,1)S(1)} %collective-permute-done.2, bf16[2,5,1536,96]{2,3,1,0:T(8,128)(2,1)S(1)} %copy-done.4), kind=kOutput, calls=%fused_computation.42 | convolution fusion | flops 616562688 | bytes 7397376 | tf_op jit(solution)/shard_map/brc,co->bro/dot_general | solution.py:24
  152.9 2.1 %fusion.49 = f32[4,512,96]{1,2,0:T(8,128)S(1)} fusion(f32[4,512,96]{1,2,0:T(8,128)S(1)} %fusion.77, f32[4,512,96]{1,2,0:T(8,128)S(1)} %fusion.26, bf16[4,2,1536]{2,1,0:T(2,128)(2,1)S(1)} %collective-permute-done.2, bf16[4,512,1536]{2,1,0:T(8,128)(2,1)S(1)} %fusion.13, bf16[2,5,1536,96]{2,3,1,0:T(8,128)(2,1)S(1)} %copy-done.4), kind=kOutput, calls=%fused_computation.57 | convolution fusion | flops 616955904 | bytes 8970240 | tf_op jit(solution)/shard_map/brc,co->bro/dot_general | solution.py:24
  155.0 2.6 %fusion.70 = bf16[1,4,512,96]{2,3,1,0:T(8,128)(2,1)S(1)} fusion(bf16[4,512,96]{1,2,0:T(8,128)(2,1)S(1)} %fusion.67, f32[4,512,96]{1,2,0:T(8,128)S(1)} %fusion.24, f32[4,512,96]{1,2,0:T(8,128)S(1)} %fusion.49, bf16[4,512,1536]{2,1,0:T(8,128)(2,1)S(1)} %fusion.13, bf16[4,2,1536]{2,1,0:T(2,128)(2,1)S(1)} %collective-permute-done.3, ...), kind=kOutput, calls=%fused_computation.66 | convolution fusion | flops 617545728 | bytes 8970240 | tf_op jit(solution)/shard_map/brc,co->bro/dot_general | solution.py:24
  (28 shorter events, 1.8 us)
Async XLA Ops:
  6.5 4.3 %copy-start.5 = (f32[2,1536]{1,0:T(2,128)S(1)}, f32[2,1536]{1,0:T(2,128)}, u32[]{:S(2)}) copy-start(f32[2,1536]{1,0:T(2,128)} %param.5) | copy-start | bytes 36868
  6.5 113.2 %all-gather.2.cloned.1.call-start = ((), (), s32[]{:S(2)}) async-start(), calls=%async_computation | async-start | bytes 6684672 | tf_op jit(solution)/shard_map/all_gather | solution.py:49
  6.5 4.6 %copy-start.1 = (bf16[4,512,1536]{2,1,0:T(8,128)(2,1)S(1)}, bf16[4,512,1536]{2,1,0:T(8,128)(2,1)}, u32[]{:S(2)}) copy-start(bf16[4,512,1536]{2,1,0:T(8,128)(2,1)} %param.3) | copy-start | bytes 18874372
  16.9 2.7 %copy-start.2 = (bf16[4,512,1536]{2,1,0:T(8,128)(2,1)}, bf16[4,512,1536]{2,1,0:T(8,128)(2,1)S(1)}, u32[]{:S(2)}) copy-start(bf16[4,512,1536]{2,1,0:T(8,128)(2,1)S(1)} %fusion.4) | copy-start | bytes 18874372
  19.6 19.1 %collective-permute-start = (bf16[4,2,1536]{2,1,0:T(2,128)(2,1)S(1)}, bf16[4,2,1536]{2,1,0:T(2,128)(2,1)S(1)}, u32[]{:S(2)}, u32[]{:S(2)}) collective-permute-start(bf16[4,2,1536]{2,1,0:T(2,128)(2,1)S(1)} %get-tuple-element.9), channel_id=1, source_target_pairs={{0,1},{1,2},{2,3},{3,4},{4,5},{5,6},{6,7},{7,8},{8,9},{9,10},{10,1... | collective-permute-start | bytes 73736 | tf_op jit(solution)/shard_map/ppermute | solution.py:14
  24.6 9.3 %collective-permute-start.1 = (bf16[4,2,1536]{2,1,0:T(2,128)(2,1)S(1)}, bf16[4,2,1536]{2,1,0:T(2,128)(2,1)S(1)}, u32[]{:S(2)}, u32[]{:S(2)}) collective-permute-start(bf16[4,2,1536]{2,1,0:T(2,128)(2,1)S(1)} %get-tuple-element.10), channel_id=1, source_target_pairs={{1,0},{2,1},{3,2},{4,3},{5,4},{6,5},{7,6},{8,7},{9,8},{10,9},{11,1... | collective-permute-start | bytes 73736 | tf_op jit(solution)/shard_map/ppermute | solution.py:15
  33.0 5.8 %slice-start = ((s8[6291456]{0:T(1024)(128)(4,1)}), s8[2097152]{0:T(1024)(128)(4,1)S(1)}, s32[]{:S(2)}) async-start(s8[6291456]{0:T(1024)(128)(4,1)} %bitcast.57), calls=%async_computation.1 | async-start | bytes 4194304
  33.9 4.9 %slice-start.1 = ((s8[6291456]{0:T(1024)(128)(4,1)}), s8[4194304]{0:T(1024)(128)(4,1)S(1)}, s32[]{:S(2)}) async-start(s8[6291456]{0:T(1024)(128)(4,1)} %bitcast.57), calls=%async_computation.2 | async-start | bytes 8388608
  41.8 3.1 %copy-start.3 = (bf16[4,512,96]{1,2,0:T(8,128)(2,1)S(1)}, bf16[4,512,96]{1,2,0:T(8,128)(2,1)}, u32[]{:S(2)}) copy-start(bf16[4,512,96]{1,2,0:T(8,128)(2,1)} %copy.18) | copy-start | bytes 1179652
  130.3 4.6 %copy-start = (bf16[4,512,1536]{2,1,0:T(8,128)(2,1)S(1)}, bf16[4,512,1536]{2,1,0:T(8,128)(2,1)}, u32[]{:S(2)}) copy-start(bf16[4,512,1536]{2,1,0:T(8,128)(2,1)} %copy.17) | copy-start | bytes 18874372
  134.9 8.4 %copy-start.4 = (bf16[2,5,1536,96]{2,3,1,0:T(8,128)(2,1)S(1)}, bf16[2,5,1536,96]{2,3,1,0:T(8,128)(2,1)}, u32[]{:S(2)}) copy-start(bf16[2,5,1536,96]{2,3,1,0:T(8,128)(2,1)} %param.4) | copy-start | bytes 8847364
  140.8 7.9 %collective-permute-start.3 = (bf16[4,2,1536]{2,1,0:T(2,128)(2,1)S(1)}, bf16[4,2,1536]{2,1,0:T(2,128)(2,1)S(1)}, u32[]{:S(2)}, u32[]{:S(2)}) collective-permute-start(bf16[4,2,1536]{2,1,0:T(2,128)(2,1)S(1)} %get-tuple-element.8), channel_id=1, source_target_pairs={{1,0},{2,1},{3,2},{4,3},{5,4},{6,5},{7,6},{8,7},{9,8},{10,9},{11,1... | collective-permute-start | bytes 73736 | tf_op jit(solution)/shard_map/ppermute | solution.py:15
  145.4 5.4 %collective-permute-start.2 = (bf16[4,2,1536]{2,1,0:T(2,128)(2,1)S(1)}, bf16[4,2,1536]{2,1,0:T(2,128)(2,1)S(1)}, u32[]{:S(2)}, u32[]{:S(2)}) collective-permute-start(bf16[4,2,1536]{2,1,0:T(2,128)(2,1)S(1)} %get-tuple-element.7), channel_id=1, source_target_pairs={{0,1},{1,2},{2,3},{3,4},{4,5},{5,6},{6,7},{7,8},{8,9},{9,10},{10,1... | collective-permute-start | bytes 73736 | tf_op jit(solution)/shard_map/ppermute | solution.py:14
Sparse Core Ops, SparseCore 0:
  49.6 70.0 all-gather.1
where the time goes:
time: 166 us; the launch traced here: 165 us
  waiting for transfers between devices  70.3 us (42%)
  matrix products  30.1 us (18%)
  other arithmetic  21 us (13%)
  local copies, waits for them, and re-layouts  17.5 us (11%)
  between operations  13.6 us (8%)
  starting transfers between devices  12.9 us (8%)
    all_gather x1, waiting for transfers between devices, local(): whole = lax.all_gather(current, 'section', axis=2, tiled=True)  70.2 us
    dot_general x10, matrix products, convolve(): jnp.einsum('brc,co->bro', padded[:, k:k + count], kernel[k], preferred_el...  30.1 us
    convert_element_type x2, other arithmetic, normed(): return jax.nn.gelu(values * scale * gain).astype(jnp.bfloat16)  11.5 us
    all_gather x1, local copies, waits for them, and re-layouts, local(): whole = lax.all_gather(current, 'section', axis=2, tiled=True)  10.6 us
    reduce_sum x2, other arithmetic, normed(): scale = lax.rsqrt(jnp.mean(values * values, axis=-1, keepdims=True) + 1e-06)  8.46 us
    ppermute x2, starting transfers between devices, with_halo(): before = lax.ppermute(last, axis, up)  8.24 us
    ppermute x2, starting transfers between devices, with_halo(): after = lax.ppermute(initial, axis, down)  4.68 us
    unnamed x17, local copies, waits for them, and re-layouts  4.3 us
  transfers between devices with their start and end apart: 5, of which 1 were waited for; matrix products, arithmetic and copies ran while one was open for 10% of the time, Pallas kernels for 0%

commit v1 on v0

--- a/solution.py
+++ b/solution.py
@@ -46,7 +46,9 @@
     current = (own.astype(jnp.float32) + conv).astype(jnp.bfloat16)
     results = [current]
     kernel = weights[1]
-    whole = lax.all_gather(current, "section", axis=2, tiled=True)
+    whole = jnp.concatenate(
+        lax.all_to_all(jnp.stack([current] * lax.axis_size("section")), "section", 0, 0), axis=2
+    )
     conv = convolve(neighbours(normed(whole, gains[1])), kernel)
     current = (current.astype(jnp.float32) + conv).astype(jnp.bfloat16)
     results.append(current)

time: 166 us -> 222 us (1.34); the launches traced: 165 us -> 218 us
  starting transfers between devices: 12.9 us -> 44.6 us
  other arithmetic: 21 us -> 38.9 us
  between operations: 13.6 us -> 0.27 us
  waiting for transfers between devices: 70.3 us -> 83.6 us
  local copies, waits for them, and re-layouts: 17.5 us -> 21.6 us
    all_to_all x0 -> x1, waiting for transfers between devices: none -> 83.6 us  [local(): lax.all_to_all(jnp.stack([current] * lax.axis_size('section')), 'section'...]
    all_gather x1 -> x0, waiting for transfers between devices: 70.2 us -> none  [local(): whole = lax.all_gather(current, 'section', axis=2, tiled=True)]
    ppermute x2, starting transfers between devices: 8.24 us -> 33.7 us  [with_halo(): before = lax.ppermute(last, axis, up)]
    convert_element_type x1, local copies, waits for them, and re-layouts: 1.05 us -> 12.6 us  [normed(): values = current.astype(jnp.float32)]
    all_gather x1 -> x0, local copies, waits for them, and re-layouts: 10.6 us -> none  [local(): whole = lax.all_gather(current, 'section', axis=2, tiled=True)]
    convert_element_type x0 -> x1, other arithmetic: none -> 9.12 us  [normed(): values = current.astype(jnp.float32)]
    convert_element_type x2 -> x3, other arithmetic: 11.5 us -> 20.6 us  [normed(): return jax.nn.gelu(values * scale * gain).astype(jnp.bfloat16)]
    all_to_all x0 -> x1, starting transfers between devices: none -> 6.81 us  [local(): lax.all_to_all(jnp.stack([current] * lax.axis_size('section')), 'section'...]
where the time goes in v1:
time: 222 us; the launch traced here: 218 us
  waiting for transfers between devices  83.6 us (38%)
  starting transfers between devices  44.6 us (20%)
  other arithmetic  38.9 us (18%)
  matrix products  29 us (13%)
  local copies, waits for them, and re-layouts  21.6 us (10%)
    all_to_all x1, waiting for transfers between devices, local(): lax.all_to_all(jnp.stack([current] * lax.axis_size('section')), 'section'...  83.6 us
    ppermute x2, starting transfers between devices, with_halo(): before = lax.ppermute(last, axis, up)  33.7 us
    dot_general x10, matrix products, convolve(): jnp.einsum('brc,co->bro', padded[:, k:k + count], kernel[k], preferred_el...  29 us
    convert_element_type x3, other arithmetic, normed(): return jax.nn.gelu(values * scale * gain).astype(jnp.bfloat16)  20.6 us
    convert_element_type x1, local copies, waits for them, and re-layouts, normed(): values = current.astype(jnp.float32)  12.6 us
    convert_element_type x1, other arithmetic, normed(): values = current.astype(jnp.float32)  9.12 us
    reduce_sum x2, other arithmetic, normed(): scale = lax.rsqrt(jnp.mean(values * values, axis=-1, keepdims=True) + 1e-06)  8.27 us
    all_to_all x1, starting transfers between devices, local(): lax.all_to_all(jnp.stack([current] * lax.axis_size('section')), 'section'...  6.81 us
  transfers between devices with their start and end apart: 5, of which 1 were waited for; matrix products, arithmetic and copies ran while one was open for 10% of the time, Pallas kernels for 0%

profile of v1, /device:TPU:1, one launch (start us, length us, event | category | flops | bytes accessed | tf_op | source)
XLA Modules:
  0.0 218.1 jit_solution(242186619643421064)
XLA Ops:
  0.0 4.2 %fusion = f32[4,512]{1,0:T(4,128)S(1)} fusion(bf16[4,512,1536]{2,1,0:T(8,128)(2,1)} %param.3), kind=kLoop, calls=%fused_computation.5 | loop fusion | flops 9435136 | bytes 6299648 | tf_op jit(solution)/shard_map/reduce_sum | solution.py:32
  4.6 5.8 %fusion.4 = bf16[4,512,1536]{2,1,0:T(8,128)(2,1)S(1)} fusion(bf16[4,512,1536]{2,1,0:T(8,128)(2,1)S(1)} %copy-done, f32[1536]{0:T(1024)S(1)} %get-tuple-element.6, f32[4,512]{1,0:T(4,128)S(1)} %add_rsqrt_fusion.1), kind=kLoop, calls=%fused_computation.9 | loop fusion | flops 37748736 | bytes 12597248 | tf_op jit(solution)/shard_map/convert_element_type | solution.py:33
  10.4 2.7 %copy-done.1 = bf16[4,512,1536]{2,1,0:T(8,128)(2,1)} copy-done((bf16[4,512,1536]{2,1,0:T(8,128)(2,1)}, bf16[4,512,1536]{2,1,0:T(8,128)(2,1)S(1)}, u32[]{:S(2)}) %copy-start.1) | copy-done | bytes 6291480
  13.1 4.9 %collective-permute-start = (bf16[4,2,1536]{2,1,0:T(2,128)(2,1)S(1)}, bf16[4,2,1536]{2,1,0:T(2,128)(2,1)S(1)}, u32[]{:S(2)}, u32[]{:S(2)}) collective-permute-start(bf16[4,2,1536]{2,1,0:T(2,128)(2,1)S(1)} %get-tuple-element.9), channel_id=1, source_target_pairs={{0,1},{1,2},{2,3},{3,4},{4,5},{5,6},{6,7},{7,8},{8,9},{9,10},{10,1... | collective-permute-start | bytes 73736 | tf_op jit(solution)/shard_map/ppermute | solution.py:14
  18.0 1.9 collective-permute-start.1
  20.0 4.8 %fusion.89 = f32[4,512,96]{1,2,0:T(8,128)S(1)} fusion(bf16[4,512,1536]{2,1,0:T(8,128)(2,1)} %copy-done.1, bf16[2,5,1536,96]{2,3,1,0:T(8,128)(2,1)} %param.4), kind=kOutput, calls=%fused_computation.82 | convolution fusion | flops 603979776 | bytes 7372800 | tf_op jit(solution)/shard_map/brc,co->bro/dot_general | solution.py:24
  27.2 4.9 %fusion.34 = f32[4,512,96]{1,2,0:T(8,128)S(1)} fusion(bf16[4,2,1536]{2,1,0:T(2,128)(2,1)S(1)} %collective-permute-done.1, bf16[4,512,1536]{2,1,0:T(8,128)(2,1)} %copy-done.1, bf16[2,5,1536,96]{2,3,1,0:T(8,128)(2,1)} %param.4), kind=kOutput, calls=%fused_computation.51 | convolution fusion | flops 616562688 | bytes 7397376 | tf_op jit(solution)/shard_map/brc,co->bro/dot_general | solution.py:24
  32.1 3.0 %fusion.36 = f32[4,512,96]{1,2,0:T(8,128)S(1)} fusion(bf16[4,512,1536]{2,1,0:T(8,128)(2,1)S(1)} %bitcast.65, bf16[4,2,1536]{2,1,0:T(2,128)(2,1)S(1)} %collective-permute-done, bf16[2,5,1536,96]{2,3,1,0:T(8,128)(2,1)} %param.4), kind=kOutput, calls=%fused_computation.54 | convolution fusion | flops 616562688 | bytes 7397376 | tf_op jit(solution)/shard_map/brc,co->bro/dot_general | solution.py:24
  35.1 3.1 %fusion.70 = f32[4,512,96]{1,2,0:T(8,128)S(1)} fusion(f32[4,512,96]{1,2,0:T(8,128)S(1)} %fusion.89, f32[4,512,96]{1,2,0:T(8,128)S(1)} %fusion.36, bf16[4,2,1536]{2,1,0:T(2,128)(2,1)S(1)} %collective-permute-done, bf16[4,512,1536]{2,1,0:T(8,128)(2,1)S(1)} %bitcast.65, bf16[2,5,1536,96]{2,3,1,0:T(8,128)(2,1)} %param.4), kind=kOutput, calls=%fused_computation.69 | convolution fusion | flops 616955904 | bytes 8970240 | tf_op jit(solution)/shard_map/brc,co->bro/dot_general | solution.py:24
  38.2 3.5 %fusion.73 = bf16[4,512,96]{1,2,0:T(8,128)(2,1)S(1)} fusion(f32[4,512,96]{1,2,0:T(8,128)S(1)} %fusion.34, f32[4,512,96]{1,2,0:T(8,128)S(1)} %fusion.70, bf16[4,512,1536]{2,1,0:T(8,128)(2,1)S(1)} %bitcast.65, bf16[4,2,1536]{2,1,0:T(2,128)(2,1)S(1)} %collective-permute-done.1, bf16[4,512,96]{1,2,0:T(8,128)(2,1)S(1)} %copy-done.2, ...), kind=kOutput, calls=%fused_computation.70 | convolution fusion | flops 617545728 | bytes 8970240 | tf_op jit(solution)/shard_map/brc,co->bro/dot_general | solution.py:24
  41.7 3.4 %stack.9 = bf16[16,4,512,96]{2,3,1,0:T(8,128)(2,1)} broadcast(bf16[4,512,96]{1,2,0:T(8,128)(2,1)S(1)} %fusion.73), dimensions={1,2,3} | broadcast | bytes 6684672 | tf_op jit(solution)/shard_map/stack | solution.py:50
  45.1 6.8 %all-to-all-start = ((bf16[16,4,512,96]{2,3,1,0:T(8,128)(2,1)}), bf16[16,4,512,96]{2,3,1,0:T(8,128)(2,1)}, u32[]{:S(2)}, u32[]{:S(2)}) async-start(bf16[16,4,512,96]{2,3,1,0:T(8,128)(2,1)} %stack.9), calls=%async_computation | async-start | bytes 12582912 | tf_op jit(solution)/shard_map/all_to_all | solution.py:50
  52.0 83.6 %all-to-all-done = bf16[16,4,512,96]{2,3,1,0:T(8,128)(2,1)} async-done(((bf16[16,4,512,96]{2,3,1,0:T(8,128)(2,1)}), bf16[16,4,512,96]{2,3,1,0:T(8,128)(2,1)}, u32[]{:S(2)}, u32[]{:S(2)}) %all-to-all-start) | async-done | bytes 6291488 | tf_op jit(solution)/shard_map/all_to_all | solution.py:50
  135.6 4.0 %multiply_reduce_fusion = f32[4,512]{1,0:T(4,128)S(1)} fusion(bf16[16,4,512,96]{2,3,1,0:T(8,128)(2,1)} %all-to-all-done), kind=kLoop, calls=%fused_computation.31 | loop fusion | flops 9435136 | bytes 6299648 | tf_op jit(solution)/shard_map/reduce_sum | solution.py:32
  139.6 9.1 %copy_convert_fusion = f32[16,4,512,96]{2,3,0,1:T(8,128)} fusion(bf16[16,4,512,96]{2,3,1,0:T(8,128)(2,1)} %all-to-all-done), kind=kLoop, calls=%fused_computation.56 | loop fusion | flops 3145728 | bytes 18874368 | tf_op jit(solution)/shard_map/convert_element_type | solution.py:31
  148.8 12.6 %copy.11 = f32[4,512,1536]{2,1,0:T(8,128)} copy(f32[4,512,1536]{1,2,0:T(8,128)} %bitcast.63) | data formatting | bytes 25165824 | tf_op jit(solution)/shard_map/convert_element_type | solution.py:31
  161.4 7.9 %fusion.17 = bf16[4,512,1536]{2,1,0:T(8,128)(2,1)S(1)} fusion(f32[4,512,1536]{2,1,0:T(8,128)} %copy.11, f32[1536]{0:T(1024)S(1)} %get-tuple-element.5, f32[4,512]{1,0:T(4,128)S(1)} %add_rsqrt_fusion), kind=kLoop, calls=%fused_computation.22 | loop fusion | flops 34603008 | bytes 18888704 | tf_op jit(solution)/shard_map/convert_element_type | solution.py:33
  169.3 2.2 %collective-permute-start.3 = (bf16[4,2,1536]{2,1,0:T(2,128)(2,1)S(1)}, bf16[4,2,1536]{2,1,0:T(2,128)(2,1)S(1)}, u32[]{:S(2)}, u32[]{:S(2)}) collective-permute-start(bf16[4,2,1536]{2,1,0:T(2,128)(2,1)S(1)} %get-tuple-element.8), channel_id=1, source_target_pairs={{1,0},{2,1},{3,2},{4,3},{5,4},{6,5},{7,6},{8,7},{9,8},{10,9},{11,1... | collective-permute-start | bytes 73736 | tf_op jit(solution)/shard_map/ppermute | solution.py:15
  171.5 6.9 %fusion.25 = bf16[4,512,16,96]{1,3,2,0:T(8,128)(2,1)S(1)} fusion(f32[16,96]{1,0:T(8,128)S(1)} %mul.122, f32[4,512]{1,0:T(4,128)S(1)} %add_rsqrt_fusion, bf16[16,4,512,96]{2,3,1,0:T(8,128)(2,1)} %all-to-all-done), kind=kLoop, calls=%fused_computation.30 | loop fusion | flops 37748736 | bytes 12597248 | tf_op jit(solution)/shard_map/convert_element_type | solution.py:33
  179.6 28.8 %collective-permute-start.2 = (bf16[4,2,1536]{2,1,0:T(2,128)(2,1)S(1)}, bf16[4,2,1536]{2,1,0:T(2,128)(2,1)S(1)}, u32[]{:S(2)}, u32[]{:S(2)}) collective-permute-start(bf16[4,2,1536]{2,1,0:T(2,128)(2,1)S(1)} %get-tuple-element.7), channel_id=1, source_target_pairs={{0,1},{1,2},{2,3},{3,4},{4,5},{5,6},{6,7},{7,8},{8,9},{9,10},{10,1... | collective-permute-start | bytes 73736 | tf_op jit(solution)/shard_map/ppermute | solution.py:14
  208.4 2.0 fusion.30
  210.5 2.0 fusion.32
  212.5 2.1 fusion.55
  214.6 2.5 %fusion.76 = bf16[1,4,512,96]{2,3,1,0:T(8,128)(2,1)S(1)} fusion(bf16[4,512,96]{1,2,0:T(8,128)(2,1)S(1)} %fusion.73, f32[4,512,96]{1,2,0:T(8,128)S(1)} %fusion.30, f32[4,512,96]{1,2,0:T(8,128)S(1)} %fusion.55, bf16[4,512,1536]{2,1,0:T(8,128)(2,1)S(1)} %fusion.17, bf16[4,2,1536]{2,1,0:T(2,128)(2,1)S(1)} %collective-permute-done.3, ...), kind=kOutput, calls=%fused_computation.73 | convolution fusion | flops 617545728 | bytes 8970240 | tf_op jit(solution)/shard_map/brc,co->bro/dot_general | solution.py:24
  (28 shorter events, 5.0 us)
Async XLA Ops:
  0.0 4.6 %copy-start = (bf16[4,512,1536]{2,1,0:T(8,128)(2,1)S(1)}, bf16[4,512,1536]{2,1,0:T(8,128)(2,1)}, u32[]{:S(2)}) copy-start(bf16[4,512,1536]{2,1,0:T(8,128)(2,1)} %param.3) | copy-start | bytes 18874372
  0.0 4.3 %copy-start.4 = (f32[2,1536]{1,0:T(2,128)S(1)}, f32[2,1536]{1,0:T(2,128)}, u32[]{:S(2)}) copy-start(f32[2,1536]{1,0:T(2,128)} %param.5) | copy-start | bytes 36868
  10.4 2.7 %copy-start.1 = (bf16[4,512,1536]{2,1,0:T(8,128)(2,1)}, bf16[4,512,1536]{2,1,0:T(8,128)(2,1)S(1)}, u32[]{:S(2)}) copy-start(bf16[4,512,1536]{2,1,0:T(8,128)(2,1)S(1)} %fusion.4) | copy-start | bytes 18874372
  13.1 19.0 %collective-permute-start = (bf16[4,2,1536]{2,1,0:T(2,128)(2,1)S(1)}, bf16[4,2,1536]{2,1,0:T(2,128)(2,1)S(1)}, u32[]{:S(2)}, u32[]{:S(2)}) collective-permute-start(bf16[4,2,1536]{2,1,0:T(2,128)(2,1)S(1)} %get-tuple-element.9), channel_id=1, source_target_pairs={{0,1},{1,2},{2,3},{3,4},{4,5},{5,6},{6,7},{7,8},{8,9},{9,10},{10,1... | collective-permute-start | bytes 73736 | tf_op jit(solution)/shard_map/ppermute | solution.py:14
  18.0 9.2 %collective-permute-start.1 = (bf16[4,2,1536]{2,1,0:T(2,128)(2,1)S(1)}, bf16[4,2,1536]{2,1,0:T(2,128)(2,1)S(1)}, u32[]{:S(2)}, u32[]{:S(2)}) collective-permute-start(bf16[4,2,1536]{2,1,0:T(2,128)(2,1)S(1)} %get-tuple-element.10), channel_id=1, source_target_pairs={{1,0},{2,1},{3,2},{4,3},{5,4},{6,5},{7,6},{8,7},{9,8},{10,9},{11,1... | collective-permute-start | bytes 73736 | tf_op jit(solution)/shard_map/ppermute | solution.py:15
  26.2 5.8 %slice-start = ((s8[6291456]{0:T(1024)(128)(4,1)}), s8[2097152]{0:T(1024)(128)(4,1)S(1)}, s32[]{:S(2)}) async-start(s8[6291456]{0:T(1024)(128)(4,1)} %bitcast.64), calls=%async_computation.1 | async-start | bytes 4194304
  27.2 4.9 %slice-start.1 = ((s8[6291456]{0:T(1024)(128)(4,1)}), s8[4194304]{0:T(1024)(128)(4,1)S(1)}, s32[]{:S(2)}) async-start(s8[6291456]{0:T(1024)(128)(4,1)} %bitcast.64), calls=%async_computation.2 | async-start | bytes 8388608
  35.1 3.1 %copy-start.2 = (bf16[4,512,96]{1,2,0:T(8,128)(2,1)S(1)}, bf16[4,512,96]{1,2,0:T(8,128)(2,1)}, u32[]{:S(2)}) copy-start(bf16[4,512,96]{1,2,0:T(8,128)(2,1)} %copy.14) | copy-start | bytes 1179652
  45.1 90.5 %all-to-all-start = ((bf16[16,4,512,96]{2,3,1,0:T(8,128)(2,1)}), bf16[16,4,512,96]{2,3,1,0:T(8,128)(2,1)}, u32[]{:S(2)}, u32[]{:S(2)}) async-start(bf16[16,4,512,96]{2,3,1,0:T(8,128)(2,1)} %stack.9), calls=%async_computation | async-start | bytes 12582912 | tf_op jit(solution)/shard_map/all_to_all | solution.py:50
  169.3 9.2 %copy-start.3 = (bf16[2,5,1536,96]{2,3,1,0:T(8,128)(2,1)S(1)}, bf16[2,5,1536,96]{2,3,1,0:T(8,128)(2,1)}, u32[]{:S(2)}) copy-start(bf16[2,5,1536,96]{2,3,1,0:T(8,128)(2,1)} %param.4) | copy-start | bytes 8847364
  169.3 39.1 %collective-permute-start.3 = (bf16[4,2,1536]{2,1,0:T(2,128)(2,1)S(1)}, bf16[4,2,1536]{2,1,0:T(2,128)(2,1)S(1)}, u32[]{:S(2)}, u32[]{:S(2)}) collective-permute-start(bf16[4,2,1536]{2,1,0:T(2,128)(2,1)S(1)} %get-tuple-element.8), channel_id=1, source_target_pairs={{1,0},{2,1},{3,2},{4,3},{5,4},{6,5},{7,6},{8,7},{9,8},{10,9},{11,1... | collective-permute-start | bytes 73736 | tf_op jit(solution)/shard_map/ppermute | solution.py:15
  179.6 30.9 %collective-permute-start.2 = (bf16[4,2,1536]{2,1,0:T(2,128)(2,1)S(1)}, bf16[4,2,1536]{2,1,0:T(2,128)(2,1)S(1)}, u32[]{:S(2)}, u32[]{:S(2)}) collective-permute-start(bf16[4,2,1536]{2,1,0:T(2,128)(2,1)S(1)} %get-tuple-element.7), channel_id=1, source_target_pairs={{0,1},{1,2},{2,3},{3,4},{4,5},{5,6},{6,7},{7,8},{8,9},{9,10},{10,1... | collective-permute-start | bytes 73736 | tf_op jit(solution)/shard_map/ppermute | solution.py:14
